TPU v7x, 32 devices: a whole 2x2x4 slice. The times are simulated.
32 devices in a mesh: dp: 8 (over z, x), mx: 2 (over y), my: 2 (over core).
Axes of the slice: x: 2, y: 2, z: 4, core: 2. Of those that a mesh axis runs over, the one named last changes fastest.
Arguments:
- layer_input: bfloat16 [32768, 768], P(('dp', 'mx', 'my')), may hold values from -6 to 6
- w_qkv: bfloat16 [768, 2304], P('mx', 'my'), may hold values from -0.21875 to 0.21875
- b_qkv: bfloat16 [2304], P(('mx', 'my')), may hold values from -3 to 3
- w_out: bfloat16 [768, 768], P('mx', 'my'), may hold values from -0.875 to 0.875
- b_out: bfloat16 [768], P(('mx', 'my')), may hold values from -2 to 2
- ln1_gain: bfloat16 [768], P(('mx', 'my')), may hold values from 0.5 to 1.5
- ln1_bias: bfloat16 [768], P(('mx', 'my')), may hold values from -2 to 2
- w_up: bfloat16 [768, 3072], P('mx', 'my'), may hold values from -0.21875 to 0.21875
- b_up: bfloat16 [3072], P(('mx', 'my')), may hold values from -3 to 3
- w_down: bfloat16 [3072, 768], P('mx', 'my'), may hold values from -0.109375 to 0.109375
- b_down: bfloat16 [768], P(('mx', 'my')), may hold values from -2 to 2
- ln2_gain: bfloat16 [768], P(('mx', 'my')), may hold values from 0.5 to 1.5
- ln2_bias: bfloat16 [768], P(('mx', 'my')), may hold values from -2 to 2
- segment_ids: int32 [32768], P(('dp', 'mx', 'my')), may hold values from 0 to 7, as said below
- doc_lengths: int32 [32, 8], P(('dp', 'mx', 'my')), may hold values from 1 to 1017, as said below
- cotangent: bfloat16 [32768, 768], P(('dp', 'mx', 'my')), may hold values from -6 to 6
Outputs:
- block_out: bfloat16 [32768, 768], P(('dp', 'mx', 'my'))
- input_grad: bfloat16 [32768, 768], P(('dp', 'mx', 'my'))
- grad_w_qkv: float32 [768, 2304], P('mx', 'my')
- grad_b_qkv: float32 [2304], P(('mx', 'my'))
- grad_w_out: float32 [768, 768], P('mx', 'my')
- grad_b_out: float32 [768], P(('mx', 'my'))
- grad_ln1_gain: float32 [768], P(('mx', 'my'))
- grad_ln1_bias: float32 [768], P(('mx', 'my'))
- grad_w_up: float32 [768, 3072], P('mx', 'my')
- grad_b_up: float32 [3072], P(('mx', 'my'))
- grad_w_down: float32 [3072, 768], P('mx', 'my')
- grad_b_down: float32 [768], P(('mx', 'my'))
- grad_ln2_gain: float32 [768], P(('mx', 'my'))
- grad_ln2_bias: float32 [768], P(('mx', 'my'))
Inputs may be any that keep to these rules, and one draw needn't show every extreme that they name: Each sequence of 1024 tokens holds exactly 8 documents back to back; segment_ids starts at 0 at each sequence's first token and rises by one at each document's first token. `doc_lengths`: A sequence's lengths sum to 1024 and are the lengths of its documents in order, as segment_ids lays them out.
All inputs are finite; a program needn't handle non-finite values.
Results may differ from a plain program's by a relative error of at most 0.018.
Values may be sent and summed in bfloat16 or wider, within the bound.
No kernel may reach another device: no remote copies, remote signals or barrier semaphores. Data moves between devices by JAX's collectives and lax.ppermute only.
A program may use at most 192 MiB of HBM per device.

v0:
```python
import math
import jax
import jax.numpy as jnp
from jax import lax
from jax.sharding import PartitionSpec as P

HD = 64
norm_eps = 1e-05


def layer_norm(resid, gain, shift):
    center = resid - jnp.mean(resid, axis=-1, keepdims=True)
    spread = jnp.mean(center * center, axis=-1, keepdims=True)
    return center * lax.rsqrt(spread + norm_eps) * gain + shift


def gelu_exact(values):
    return jax.nn.gelu(values, approximate=False)


def geometry(segment, spans):
    doc_count = spans.shape[0]
    member = segment[:, None] == jnp.arange(doc_count, dtype=jnp.int32)[None, :]
    doc_span = jnp.sum(jnp.where(member, spans[None, :], 0), axis=1)
    length = segment.shape[0]
    places = jnp.arange(length, dtype=jnp.int32)
    angle = 0.5 * math.pi * places.astype(jnp.float32) / doc_span.astype(jnp.float32)
    causal = places[:, None] >= places[None, :]
    keep_mask = jnp.where((segment[:, None] == segment[None, :]) & causal, 1.0, 0.0).astype(
        jnp.float32
    )
    return (jnp.cos(angle), jnp.sin(angle), keep_mask)


def project_forward(operand, matrix):
    rows_here = operand.shape[0]
    grid_rows, grid_cols, row_size, col_size = matrix.shape
    result = jnp.einsum(
        "tid,ijdn->tjn",
        operand.reshape(rows_here, grid_rows, row_size),
        matrix,
        preferred_element_type=jnp.float32,
    )
    return result.reshape(rows_here, grid_cols * col_size)


def project_back(grad_rows, matrix):
    rows_here = grad_rows.shape[0]
    grid_rows, grid_cols, row_size, col_size = matrix.shape
    result = jnp.einsum(
        "tjn,ijdn->tid",
        grad_rows.reshape(rows_here, grid_cols, col_size),
        matrix,
        preferred_element_type=jnp.float32,
    )
    return result.reshape(rows_here, grid_rows * row_size)


def weight_grad(operand, grad_rows, matrix):
    rows_here = operand.shape[0]
    grid_rows, grid_cols, row_size, col_size = matrix.shape
    result = jnp.einsum(
        "tid,tjn->ijdn",
        operand.reshape(rows_here, grid_rows, row_size),
        grad_rows.reshape(rows_here, grid_cols, col_size),
        preferred_element_type=jnp.float32,
    )
    return result.reshape(grid_rows * grid_cols, row_size, col_size)


def fetch_weights(
    w_qkv, w_out, w_up, w_down, b_qkv, b_out, ln1_gain, ln1_bias, b_up, b_down, ln2_gain, ln2_bias
):
    fetched = (
        lax.all_gather(w_qkv[None], ("mx", "my"), axis=0, tiled=True),
        lax.all_gather(w_out[None], ("mx", "my"), axis=0, tiled=True),
        lax.all_gather(w_up[None], ("mx", "my"), axis=0, tiled=True),
        lax.all_gather(w_down[None], ("mx", "my"), axis=0, tiled=True),
        lax.all_gather(b_qkv, ("mx", "my"), axis=0, tiled=True),
        lax.all_gather(b_out, ("mx", "my"), axis=0, tiled=True),
        lax.all_gather(ln1_gain, ("mx", "my"), axis=0, tiled=True),
        lax.all_gather(ln1_bias, ("mx", "my"), axis=0, tiled=True),
        lax.all_gather(b_up, ("mx", "my"), axis=0, tiled=True),
        lax.all_gather(b_down, ("mx", "my"), axis=0, tiled=True),
        lax.all_gather(ln2_gain, ("mx", "my"), axis=0, tiled=True),
        lax.all_gather(ln2_bias, ("mx", "my"), axis=0, tiled=True),
    )
    grid_rows = lax.axis_size("mx")
    grid_cols = lax.axis_size("my")
    matrices = tuple(
        (
            piece.reshape(grid_rows, grid_cols, piece.shape[1], piece.shape[2])
            for piece in fetched[:4]
        )
    )
    return (matrices, fetched[4:], "stack")


def reduce_grads(grads):
    summed = (
        lax.psum_scatter(
            grads[0].astype(jnp.bfloat16), ("mx", "my"), scatter_dimension=0, tiled=True
        ).astype(jnp.float32),
        lax.psum_scatter(
            grads[1].astype(jnp.bfloat16), ("mx", "my"), scatter_dimension=0, tiled=True
        ).astype(jnp.float32),
        lax.psum_scatter(
            grads[2].astype(jnp.bfloat16), ("mx", "my"), scatter_dimension=0, tiled=True
        ).astype(jnp.float32),
        lax.psum_scatter(
            grads[3].astype(jnp.bfloat16), ("mx", "my"), scatter_dimension=0, tiled=True
        ).astype(jnp.float32),
        lax.psum_scatter(
            grads[4].astype(jnp.bfloat16), ("mx", "my"), scatter_dimension=0, tiled=True
        ).astype(jnp.float32),
        lax.psum_scatter(
            grads[5].astype(jnp.bfloat16), ("mx", "my"), scatter_dimension=0, tiled=True
        ).astype(jnp.float32),
        lax.psum_scatter(
            grads[6].astype(jnp.bfloat16), ("mx", "my"), scatter_dimension=0, tiled=True
        ).astype(jnp.float32),
        lax.psum_scatter(
            grads[7].astype(jnp.bfloat16), ("mx", "my"), scatter_dimension=0, tiled=True
        ).astype(jnp.float32),
        lax.psum_scatter(
            grads[8].astype(jnp.bfloat16), ("mx", "my"), scatter_dimension=0, tiled=True
        ).astype(jnp.float32),
        lax.psum_scatter(
            grads[9].astype(jnp.bfloat16), ("mx", "my"), scatter_dimension=0, tiled=True
        ).astype(jnp.float32),
        lax.psum_scatter(
            grads[10].astype(jnp.bfloat16), ("mx", "my"), scatter_dimension=0, tiled=True
        ).astype(jnp.float32),
        lax.psum_scatter(
            grads[11].astype(jnp.bfloat16), ("mx", "my"), scatter_dimension=0, tiled=True
        ).astype(jnp.float32),
    )
    blocks = tuple((piece[0] for piece in summed[:4])) + tuple(summed[4:])
    return (
        lax.psum(blocks[0].astype(jnp.bfloat16), "dp").astype(jnp.float32),
        lax.psum(blocks[1].astype(jnp.bfloat16), "dp").astype(jnp.float32),
        lax.psum(blocks[2].astype(jnp.bfloat16), "dp").astype(jnp.float32),
        lax.psum(blocks[3].astype(jnp.bfloat16), "dp").astype(jnp.float32),
        lax.psum(blocks[4].astype(jnp.bfloat16), "dp").astype(jnp.float32),
        lax.psum(blocks[5].astype(jnp.bfloat16), "dp").astype(jnp.float32),
        lax.psum(blocks[6].astype(jnp.bfloat16), "dp").astype(jnp.float32),
        lax.psum(blocks[7].astype(jnp.bfloat16), "dp").astype(jnp.float32),
        lax.psum(blocks[8].astype(jnp.bfloat16), "dp").astype(jnp.float32),
        lax.psum(blocks[9].astype(jnp.bfloat16), "dp").astype(jnp.float32),
        lax.psum(blocks[10].astype(jnp.bfloat16), "dp").astype(jnp.float32),
        lax.psum(blocks[11].astype(jnp.bfloat16), "dp").astype(jnp.float32),
    )


def body(
    layer_input,
    w_qkv,
    b_qkv,
    w_out,
    b_out,
    ln1_gain,
    ln1_bias,
    w_up,
    b_up,
    w_down,
    b_down,
    ln2_gain,
    ln2_bias,
    segment_ids,
    doc_lengths,
    cotangent,
):
    seqs_here = doc_lengths.shape[0]
    tokens = layer_input.shape[0]
    length = tokens // seqs_here
    model_width = layer_input.shape[1]
    head_count = model_width // HD
    cosine, sine, keep_mask = jax.vmap(geometry)(
        segment_ids.reshape(seqs_here, length), doc_lengths
    )
    cos_col = cosine[:, :, None, None]
    sin_col = sine[:, :, None, None]
    matrices, vectors, layout = fetch_weights(
        w_qkv,
        w_out,
        w_up,
        w_down,
        b_qkv,
        b_out,
        ln1_gain,
        ln1_bias,
        b_up,
        b_down,
        ln2_gain,
        ln2_bias,
    )
    m_qkv, m_out, m_up, m_down = matrices
    f_bqkv, f_bout, f_gain1, f_bias1, f_bup, f_bdown, f_gain2, f_bias2 = tuple(
        (item.astype(jnp.float32) for item in vectors)
    )
    proj = project_forward(layer_input, m_qkv) + f_bqkv
    pre_query = proj[:, :model_width].reshape(seqs_here, length, head_count, HD)
    pre_key = proj[:, model_width : 2 * model_width].reshape(seqs_here, length, head_count, HD)
    query = jax.nn.relu(pre_query) * 0.125
    keyed = jax.nn.relu(pre_key)
    q_feat = jnp.moveaxis(
        jnp.concatenate([query * cos_col, query * sin_col], axis=-1).astype(jnp.bfloat16), 2, 0
    )
    k_feat = jnp.moveaxis(
        jnp.concatenate([keyed * cos_col, keyed * sin_col], axis=-1).astype(jnp.bfloat16), 2, 0
    )
    v_bf = jnp.moveaxis(
        proj[:, 2 * model_width :].reshape(seqs_here, length, head_count, HD).astype(jnp.bfloat16),
        2,
        0,
    )

    def attend(pieces):
        q_part, k_part, v_part = pieces
        scores = (
            jnp.einsum("sid,sjd->sij", q_part, k_part, preferred_element_type=jnp.float32)
            * keep_mask
        )
        denom = jnp.maximum(jnp.sum(scores, axis=-1), 1.0)
        numer = jnp.einsum(
            "sij,sjd->sid", scores.astype(jnp.bfloat16), v_part, preferred_element_type=jnp.float32
        )
        return (numer, denom)

    numer, denom = lax.map(attend, (q_feat, k_feat, v_bf))
    attn_full = numer / denom[..., None]
    attn = jnp.moveaxis(attn_full, 0, 2).reshape(tokens, model_width).astype(jnp.bfloat16)
    branch = project_forward(attn, m_out) + f_bout
    resid_one = layer_input.astype(jnp.float32) + branch
    hidden, pull_one = jax.vjp(layer_norm, resid_one, f_gain1, f_bias1)
    hidden_bf = hidden.astype(jnp.bfloat16)
    upward = project_forward(hidden_bf, m_up) + f_bup
    action, pull_gelu = jax.vjp(gelu_exact, upward)
    action_bf = action.astype(jnp.bfloat16)
    downward = project_forward(action_bf, m_down) + f_bdown
    result, pull_two = jax.vjp(layer_norm, hidden + downward, f_gain2, f_bias2)
    d_resid_two, grad_gain2, grad_bias2 = pull_two(cotangent.astype(jnp.float32))
    d_down = d_resid_two.astype(jnp.bfloat16)
    grad_bdown = jnp.sum(d_down, axis=0, dtype=jnp.float32)
    grad_wdown = weight_grad(action_bf, d_down, m_down)
    d_action = project_back(d_down, m_down)
    (d_up_full,) = pull_gelu(d_action)
    d_up = d_up_full.astype(jnp.bfloat16)
    grad_bup = jnp.sum(d_up, axis=0, dtype=jnp.float32)
    grad_wup = weight_grad(hidden_bf, d_up, m_up)
    d_hidden = project_back(d_up, m_up) + d_resid_two
    d_resid_one, grad_gain1, grad_bias1 = pull_one(d_hidden)
    d_branch = d_resid_one.astype(jnp.bfloat16)
    grad_bout = jnp.sum(d_branch, axis=0, dtype=jnp.float32)
    grad_wout = weight_grad(attn, d_branch, m_out)
    d_attn = jnp.moveaxis(
        project_back(d_branch, m_out).reshape(seqs_here, length, head_count, HD), 2, 0
    )
    d_denom = jnp.where(denom > 1.0, -jnp.sum(d_attn * attn_full, axis=-1) / denom, 0.0)
    d_numer = (d_attn / denom[..., None]).astype(jnp.bfloat16)

    def attend_back(pieces):
        q_part, k_part, v_part, numer_grad, denom_grad = pieces
        scores = (
            jnp.einsum("sid,sjd->sij", q_part, k_part, preferred_element_type=jnp.float32)
            * keep_mask
        )
        score_grad = (
            jnp.einsum("sid,sjd->sij", numer_grad, v_part, preferred_element_type=jnp.float32)
            + denom_grad[..., None]
        )
        score_grad = jnp.where(keep_mask > 0.0, score_grad, 0.0).astype(jnp.bfloat16)
        q_grad = jnp.einsum("sij,sjd->sid", score_grad, k_part, preferred_element_type=jnp.float32)
        k_grad = jnp.einsum("sij,sid->sjd", score_grad, q_part, preferred_element_type=jnp.float32)
        v_grad = jnp.einsum(
            "sij,sid->sjd",
            scores.astype(jnp.bfloat16),
            numer_grad,
            preferred_element_type=jnp.float32,
        )
        return (q_grad, k_grad, v_grad)

    d_qfeat, d_kfeat, d_value = lax.map(attend_back, (q_feat, k_feat, v_bf, d_numer, d_denom))
    d_qfeat = jnp.moveaxis(d_qfeat, 0, 2)
    d_kfeat = jnp.moveaxis(d_kfeat, 0, 2)
    d_query = (d_qfeat[..., :HD] * cos_col + d_qfeat[..., HD:] * sin_col) * 0.125
    d_query = jnp.where(pre_query > 0.0, d_query, 0.0)
    d_keyed = d_kfeat[..., :HD] * cos_col + d_kfeat[..., HD:] * sin_col
    d_keyed = jnp.where(pre_key > 0.0, d_keyed, 0.0)
    d_valued = jnp.moveaxis(d_value, 0, 2)
    d_proj = jnp.concatenate(
        [
            d_query.reshape(tokens, model_width),
            d_keyed.reshape(tokens, model_width),
            d_valued.reshape(tokens, model_width),
        ],
        axis=1,
    ).astype(jnp.bfloat16)
    grad_bqkv = jnp.sum(d_proj, axis=0, dtype=jnp.float32)
    grad_wqkv = weight_grad(layer_input, d_proj, m_qkv)
    input_grad = (project_back(d_proj, m_qkv) + d_resid_one).astype(jnp.bfloat16)
    totals = reduce_grads(
        (
            grad_wqkv,
            grad_wout,
            grad_wup,
            grad_wdown,
            grad_bqkv,
            grad_bout,
            grad_gain1,
            grad_bias1,
            grad_bup,
            grad_bdown,
            grad_gain2,
            grad_bias2,
        )
    )
    return (
        result.astype(jnp.bfloat16),
        input_grad,
        totals[0],
        totals[4],
        totals[1],
        totals[5],
        totals[6],
        totals[7],
        totals[2],
        totals[8],
        totals[3],
        totals[9],
        totals[10],
        totals[11],
    )


def solution(mesh):
    return jax.shard_map(
        body,
        mesh=mesh,
        in_specs=(
            P(("dp", "mx", "my"), None),
            P("mx", "my"),
            P(("mx", "my")),
            P("mx", "my"),
            P(("mx", "my")),
            P(("mx", "my")),
            P(("mx", "my")),
            P("mx", "my"),
            P(("mx", "my")),
            P("mx", "my"),
            P(("mx", "my")),
            P(("mx", "my")),
            P(("mx", "my")),
            P(("dp", "mx", "my")),
            P(("dp", "mx", "my"), None),
            P(("dp", "mx", "my"), None),
        ),
        out_specs=(
            P(("dp", "mx", "my"), None),
            P(("dp", "mx", "my"), None),
            P("mx", "my"),
            P(("mx", "my")),
            P("mx", "my"),
            P(("mx", "my")),
            P(("mx", "my")),
            P(("mx", "my")),
            P("mx", "my"),
            P(("mx", "my")),
            P("mx", "my"),
            P(("mx", "my")),
            P(("mx", "my")),
            P(("mx", "my")),
        ),
        check_vma=False,
    )
```

profile of v0, /device:TPU:0, one launch (start us, length us, event | category | flops | bytes accessed | tf_op | source)
XLA Modules:
  0.0 724.5 jit_solution(8829298997838399889)
XLA Ops:
  14.9 13.2 %all-reduce.18 = (bf16[2304]{0:T(1024)(128)(2,1)S(1)}, bf16[768]{0:T(1024)(128)(2,1)S(1)}, bf16[768]{0:T(1024)(128)(2,1)S(1)}, bf16[768]{0:T(1024)(128)(2,1)S(1)...) all-reduce(bf16[2304]{0:T(1024)(128)(2,1)S(1)} %dynamic-update-slic, ...), channel_id=1, replica_groups=mesh['dp'=8,'mx'=2,'my'=2] {'mx','my'}, use_global_device_ids=true, to_apply=%add | all-reduce | flops 6144 | bytes 24576
  32.3 5.4 all-gather.4
  44.7 17.7 %all-gather.10.cloned.1.call-done = bf16[1536,1152]{1,0:T(8,128)(2,1)} async-done(((bf16[384,1152]{1,0:T(8,128)(2,1)}), bf16[1536,1152]{1,0:T(8,128)(2,1)}) %all-gather.10.cloned.1.call-update) | async-done | bytes 3538960 | tf_op jit(solution)/shard_map/all_gather | solution.py:75
  62.4 4.5 copy.202
  67.0 5.3 bitcast_add_fusion.1
  72.3 3.3 slice_maximum_fusion
  81.7 3.6 copy.204
  85.4 4.7 fusion.106
  90.4 2.8 copy.208
  95.7 2.8 copy.207
  100.3 2.8 copy.209
  103.1 52.9 %while.30 = (s32[]{:T(128)}, f32[12,1,1024,64]{2,3,1,0:T(8,128)}, f32[12,1,1024]{2,1,0:T(1,128)S(1)}, bf16[12,1,1024,128]{3,2,1,0:T(8,128)(2,1)}, bf16[12,1,1024...) while((s32[]{:T(128)}, f32[12,1,1024,64]{2,3,1,0:T(8,128)}, ...), condition=%wide.region_3.4_spmd.clone.clone, body=%wide.region_1.3_spmd.clone.sunk.clone | while | flops 415236096 | bytes 9476177 | solution.py:230
  156.6 4.8 slice_compare_fusion.1
  161.4 2.9 copy.217
  164.3 3.2 copy.231
  173.4 7.2 copy.215
  180.6 4.9 copy.219
  185.6 6.6 copy.213
  192.2 5.0 copy.221
  197.3 33.6 %multiply_convert_fusion = (bf16[1024,3072]{1,0:T(8,128)(2,1)S(1)}, f32[1024,3072]{1,0:T(8,128)}, f32[1024,3072,1]{1,0,2:T(8,128)}) fusion(f32[3072]{0:T(1024)S(1)} %bitcast.428, bf16[1024,2,384]{0,2,1:T(8,128)(2,1)S(1)} %bitcast.412, bf16[3072,384,2]{1,0,2:T(8,128)(2,1)S(1)} %bitcast.400), kind=kOutput, calls=%fused_computation.69 | convolution fusion | flops 5039456256 | bytes 37761024 | tf_op jit(solution)/shard_map/tid,ijdn->tjn/dot_general | solution.py:38
  231.0 5.3 fusion.127
  239.4 2.9 fusion.120
  242.3 16.7 %fusion.128 = (bf16[3072]{0:T(1024)(128)(2,1)S(1)}, bf16[1024,3072]{1,0:T(8,128)(2,1)}) fusion(f32[1024,3072]{1,0:T(8,128)} %get-tuple-element.376, bf16[1024,2,384]{0,2,1:T(8,128)(2,1)} %bitcast.414, bf16[3072,2,384]{2,0,1:T(8,128)(2,1)} %bitcast.396, f32[3072]{0:T(1024)S(1)} %bitcast.429, f32[1024,3072,1]{1,0,2:T(8,128)} %get-tuple-element.401), kind=kOutput, calls=%fused_computation.190 | convolution fusion | flops 4882166784 | bytes 37767168 | tf_op jit(solution)/shard_map/tjn,ijdn->tid/dot_general | solution.py:50
  259.0 11.3 %multiply_reduce_fusion = (bf16[768]{0:T(1024)(128)(2,1)S(1)}, f32[1024]{0:T(1024)S(1)}, bf16[768]{0:T(1024)(128)(2,1)S(1)}, f32[1024,768]{0,1:T(8,128)S(1)}) fusion(f32[1024,768]{0,1:T(8,128)S(1)} %copy-done.1, f32[1024]{0:T(1024)S(1)} %copy-done.33, f32[1024]{0:T(1024)S(1)} %copy-done.29, f32[768]{0:T(1024)S(1)} %copy-done.31, ...), kind=kOutput, calls=%fused_computation.135 | convolution fusion | flops 4845204480 | bytes 22057984 | tf_op jit(solution)/shard_map/tjn,ijdn->tid/dot_general | solution.py:50
  276.8 2.6 copy.239
  279.5 5.6 fusion.97
  285.2 117.9 %while.31 = (s32[]{:T(128)}, f32[12,1,1024,128]{2,3,0,1:T(8,128)}, f32[12,1,1024,128]{2,3,0,1:T(8,128)}, bf16[12,1,1024,64]{2,3,1,0:T(8,128)(2,1)}, bf16[12,1,10...) while((s32[]{:T(128)}, f32[12,1,1024,128]{2,3,0,1:T(8,128)}, ...), condition=%wide.region_14.15_spmd.clone.clone, body=%wide.region_13.14_spmd.clone.sunk.clone | while | flops 1088421888 | bytes 9208937 | solution.py:283
  287.4 2.6 fusion.194
  292.3 2.8 fusion.196
  302.0 2.8 fusion.196
  311.8 2.8 fusion.196
  316.8 2.6 fusion.194
  321.7 2.8 fusion.196
  326.7 2.6 fusion.194
  331.5 2.8 fusion.196
  341.3 2.8 fusion.196
  346.3 2.6 fusion.194
  351.1 2.8 fusion.196
  356.1 2.6 fusion.194
  361.0 2.8 fusion.196
  365.9 2.6 fusion.194
  370.8 2.8 fusion.196
  375.8 2.6 fusion.194
  380.6 2.8 fusion.196
  390.4 2.8 fusion.196
  395.4 2.6 fusion.194
  400.2 2.8 fusion.196
  403.0 6.3 fusion.95
  412.5 5.2 fusion.84
  417.7 5.8 copy.237
  423.6 9.1 %convert_bitcast_fusion = bf16[2,2,1536,384]{2,3,0,1:T(8,128)(2,1)} fusion(bf16[1024,2,384,1]{0,2,3,1:T(8,128)(2,1)} %bitcast.415, bf16[128,2,8,1536]{3,2,1,0:T(8,128)(2,1)} %bitcast.432), kind=kOutput, calls=%fused_computation.99 | convolution fusion | flops 4834197504 | bytes 12582912 | tf_op jit(solution)/shard_map/tid,tjn->ijdn/dot_general | solution.py:62
  432.7 6.9 copy.244
  439.6 15.3 %reshape.597 = bf16[1024,2,1536]{2,1,0:T(2,128)(2,1)} reshape(bf16[1024,3072]{1,0:T(8,128)(2,1)} %get-tuple-element.406) | data formatting | bytes 12582912 | tf_op jit(solution)/shard_map/reshape | solution.py:52
  454.9 10.6 %convert_bitcast_fusion.1 = bf16[2,2,384,1536]{2,3,0,1:T(8,128)(2,1)} fusion(bf16[1024,2,384,1]{0,2,1,3:T(8,128)(2,1)} %bitcast.413, bf16[1024,2,1536,1]{2,1,0,3:T(2,128)(2,1)} %bitcast.386), kind=kOutput, calls=%fused_computation.100 | convolution fusion | flops 4834197504 | bytes 12582912 | tf_op jit(solution)/shard_map/tid,tjn->ijdn/dot_general | solution.py:62
  465.5 6.7 copy.242
  472.3 42.8 %reduce-scatter.11.cloned.1.call-done = bf16[1,1536,384]{2,1,0:T(8,128)(2,1)} async-done(((bf16[4,1536,384]{2,1,0:T(8,128)(2,1)}), bf16[1,1536,384]{2,1,0:T(8,128)(2,1)}) %reduce-scatter.11.cloned.1.call-update) | async-done | bytes 1179664 | tf_op jit(solution)/shard_map/reduce_scatter | solution.py:110
  515.0 50.6 %reduce-scatter.9.cloned.1.call-done = bf16[1,384,1536]{2,1,0:T(8,128)(2,1)} async-done(((bf16[4,384,1536]{2,1,0:T(8,128)(2,1)}), bf16[1,384,1536]{2,1,0:T(8,128)(2,1)}) %reduce-scatter.9.cloned.1.call-update) | async-done | bytes 1179664 | tf_op jit(solution)/shard_map/reduce_scatter | solution.py:107
  569.5 4.0 copy.233
  573.6 10.7 %all-reduce.17 = (bf16[768]{0:T(1024)(128)(2,1)S(1)}, bf16[2304]{0:T(1024)(128)(2,1)S(1)}, bf16[768]{0:T(1024)(128)(2,1)S(1)}, bf16[768]{0:T(1024)(128)(2,1)S(1)...) all-reduce(bf16[768]{0:T(1024)(128)(2,1)S(1)} %dynamic-update-slice, ...), channel_id=1, replica_groups=mesh['dp'=8,'mx'=2,'my'=2] {'mx','my'}, use_global_device_ids=true, to_apply=%add.6 | all-reduce | flops 10752 | bytes 43008
  584.9 23.7 %all-reduce.15 = (bf16[576]{0:T(1024)(128)(2,1)S(1)}, bf16[192]{0:T(256)(128)(2,1)S(1)}, bf16[192]{0:T(256)(128)(2,1)S(1)}, bf16[192]{0:T(256)(128)(2,1)S(1)}, b...) all-reduce(bf16[576]{0:T(1024)(128)(2,1)S(1)} %dynamic-slice.8, ...), channel_id=1, replica_groups=mesh['dp'=8,'mx'=2,'my'=2] {'dp'}, use_global_device_ids=true, to_apply=%region_19.20 | all-reduce | flops 2496 | bytes 9984 | tf_op jit(solution)/shard_map/psum | solution.py:144
  613.1 9.3 %fusion.98 = bf16[1024,768]{0,1:T(8,128)(2,1)} fusion(f32[1024,768]{0,1:T(8,128)} %copy-done.4, bf16[768,2,1152]{2,0,1:T(8,128)(2,1)} %bitcast.404, bf16[1024,2,1152]{0,2,1:T(8,128)(2,1)} %bitcast.394, f32[1024]{0:T(1024)S(1)} %negate_multiply_fusion.1), kind=kOutput, calls=%fused_computation.128 | convolution fusion | flops 3626237952 | bytes 12980224 | tf_op jit(solution)/shard_map/tjn,ijdn->tid/dot_general | solution.py:50
  622.4 2.6 copy.246
  629.3 81.4 %all-reduce.21.cloned.1.call-done = (bf16[384,1152]{1,0:T(8,128)(2,1)}, bf16[384,384]{1,0:T(8,128)(2,1)}, bf16[384,1536]{1,0:T(8,128)(2,1)}, bf16[1536,384]{1,0:T(8,128)(2,1)}) async-done(((bf16[384,1152]{1,0:T(8,128)(2,1)}, bf16[384,384]{1,0:T(8,128)(2,1)}, bf16[384,1536]{1,0:T(8,128)(2,1)}, bf16[1536,384]{1,0:T(8,128)(2,1)}), (bf16[384,1152]{1,0:T(8,128)(2,1)}, bf16[384,384]{1,0:T(8,128)(2,1)}, ...) | async-done | bytes 3538960 | tf_op jit(solution)/shard_map/psum | solution.py:140
  710.7 3.1 convert_element_type.319
  (322 shorter events, 178.3 us)
Async XLA Ops:
  7.2 4.4 copy-start.51
  7.2 6.2 copy-start.55
  7.2 6.5 copy-start.56
  7.2 6.7 copy-start.57
  7.2 6.9 copy-start.58
  7.2 7.2 copy-start.59
  7.2 7.4 %copy-start.52 = (bf16[576]{0:T(1024)(128)(2,1)S(1)}, bf16[576]{0:T(1024)(128)(2,1)}, u32[]{:S(2)}) copy-start(bf16[576]{0:T(1024)(128)(2,1)} %param.22) | copy-start | bytes 3460
  7.3 21.4 %copy-start.54 = (s32[1,8]{1,0:T(1,128)S(1)}, s32[1,8]{1,0:T(1,128)}, u32[]{:S(2)}) copy-start(s32[1,8]{1,0:T(1,128)} %param.34) | copy-start | bytes 100
  7.3 21.4 %copy-start.48 = (s32[1024]{0:T(1024)S(1)}, s32[1024]{0:T(1024)}, u32[]{:S(2)}) copy-start(s32[1024]{0:T(1024)} %param.33) | copy-start | bytes 12292
  7.3 22.7 %copy-start.12 = (bf16[1024,768]{1,0:T(8,128)(2,1)S(1)}, bf16[1024,768]{1,0:T(8,128)(2,1)}, u32[]{:S(2)}) copy-start(bf16[1024,768]{1,0:T(8,128)(2,1)} %param.20) | copy-start | bytes 4718596
  7.3 33.8 %all-gather.12.cloned.1.call-start = ((), (), s32[]{:S(2)}) async-start(), calls=%async_computation.9 | async-start | bytes 1474560 | tf_op jit(solution)/shard_map/all_gather | solution.py:76
  8.0 54.4 %all-gather.10.cloned.1.call-start = ((), (), s32[]{:S(2)}) async-start(), calls=%async_computation.8 | async-start | bytes 4423680 | tf_op jit(solution)/shard_map/all_gather | solution.py:75
  8.8 164.6 %all-gather.16.cloned.1.call-start = ((), (), s32[]{:S(2)}) async-start(), calls=%async_computation.11 | async-start | bytes 5898240 | tf_op jit(solution)/shard_map/all_gather | solution.py:78
  9.5 22.7 %copy-start.53 = (bf16[768]{0:T(1024)(128)(2,1)S(1)}, bf16[768]{0:T(1024)(128)(2,1)}, u32[]{:S(2)}) copy-start(bf16[768]{0:T(1024)(128)(2,1)} %param.28) | copy-start | bytes 4612
  9.5 29.9 %copy-start.5 = (bf16[1024,768]{1,0:T(8,128)(2,1)S(1)}, bf16[1024,768]{1,0:T(8,128)(2,1)}, u32[]{:S(2)}) copy-start(bf16[1024,768]{1,0:T(8,128)(2,1)} %param.35) | copy-start | bytes 4718596
  9.5 176.1 %all-gather.14.cloned.1.call-start = ((), (), s32[]{:S(2)}) async-start(), calls=%async_computation.10 | async-start | bytes 5898240 | tf_op jit(solution)/shard_map/all_gather | solution.py:77
  10.1 462.1 %reduce-scatter.7.cloned.1.call-start = ((), (), s32[]{:S(2)}) async-start(), calls=%async_computation.5 | async-start | bytes 1474560 | tf_op jit(solution)/shard_map/reduce_scatter | solution.py:104
  29.4 55.9 %copy-start.36 = (f32[1024]{0:T(1024)}, f32[1024]{0:T(1024)S(1)}, u32[]{:S(2)}) copy-start(f32[1024]{0:T(1024)S(1)} %get-tuple-element.393) | copy-start | bytes 12292
  29.4 55.9 %copy-start.38 = (f32[1024]{0:T(1024)}, f32[1024]{0:T(1024)S(1)}, u32[]{:S(2)}) copy-start(f32[1024]{0:T(1024)S(1)} %get-tuple-element.396) | copy-start | bytes 12292
  31.6 140.0 %copy-start.30 = (f32[768]{0:T(1024)}, f32[768]{0:T(1024)S(1)}, u32[]{:S(2)}) copy-start(f32[768]{0:T(1024)S(1)} %convert_element_type.283) | copy-start | bytes 9220
  41.1 2.5 copy-start.9
  72.3 5.8 copy-start.3
  81.7 3.6 copy-start.40
  100.3 2.8 copy-start.24
  100.3 2.8 copy-start.49
  156.6 10.9 %copy-start.22 = (f32[12,1,1024]{2,0,1:T(8,128)}, f32[12,1,1024]{2,0,1:T(8,128)S(1)}, u32[]{:S(2)}) copy-start(f32[12,1,1024]{2,0,1:T(8,128)S(1)} %copy.322) | copy-start | bytes 147460
  161.4 6.1 copy-start.10
  164.3 3.7 copy-start.47
  168.0 3.2 copy-start.16
  171.7 9.0 %copy-start.34 = (f32[1024]{0:T(1024)}, f32[1024]{0:T(1024)S(1)}, u32[]{:S(2)}) copy-start(f32[1024]{0:T(1024)S(1)} %multiply_reduce_fusion.3) | copy-start | bytes 12292
  172.9 7.8 %copy-start.32 = (f32[1024]{0:T(1024)}, f32[1024]{0:T(1024)S(1)}, u32[]{:S(2)}) copy-start(f32[1024]{0:T(1024)S(1)} %fusion.115) | copy-start | bytes 12292
  173.4 23.8 %copy-start.15 = (bf16[1024,768]{0,1:T(8,128)(2,1)}, bf16[1024,768]{0,1:T(8,128)(2,1)S(1)}, u32[]{:S(2)}) copy-start(bf16[1024,768]{0,1:T(8,128)(2,1)S(1)} %fusion.101) | copy-start | bytes 4718596
  192.2 5.0 copy-start.8
  192.2 5.0 copy-start.43
  192.2 38.7 %slice-start = ((s8[4718592]{0:T(1024)(128)(4,1)}), s8[524288]{0:T(1024)(128)(4,1)S(1)}, s32[]{:S(2)}) async-start(s8[4718592]{0:T(1024)(128)(4,1)} %bitcast.397), calls=%async_computation.13 | async-start | bytes 1048576
  197.2 33.7 %copy-start.1 = (f32[1024,768]{0,1:T(8,128)S(1)}, f32[1024,768]{0,1:T(8,128)}, u32[]{:S(2)}) copy-start(f32[1024,768]{0,1:T(8,128)} %copy-done) | copy-start | bytes 9437188
  197.2 33.7 %slice-start.1 = ((s8[4718592]{0:T(1024)(128)(4,1)}), s8[4194304]{0:T(1024)(128)(4,1)S(1)}, s32[]{:S(2)}) async-start(s8[4718592]{0:T(1024)(128)(4,1)} %bitcast.397), calls=%async_computation.14 | async-start | bytes 8388608
  197.3 33.7 %copy-start.29 = (f32[1024]{0:T(1024)S(1)}, f32[1024]{0:T(1024)}, u32[]{:S(2)}) copy-start(f32[1024]{0:T(1024)} %copy-done.28) | copy-start | bytes 12292
  197.3 33.7 %copy-start.31 = (f32[768]{0:T(1024)S(1)}, f32[768]{0:T(1024)}, u32[]{:S(2)}) copy-start(f32[768]{0:T(1024)} %copy-done.30) | copy-start | bytes 9220
  197.3 33.7 %copy-start.33 = (f32[1024]{0:T(1024)S(1)}, f32[1024]{0:T(1024)}, u32[]{:S(2)}) copy-start(f32[1024]{0:T(1024)} %copy-done.32) | copy-start | bytes 12292
  197.3 33.7 %copy-start.42 = (f32[768]{0:T(1024)S(1)}, f32[768]{0:T(1024)}, u32[]{:S(2)}) copy-start(f32[768]{0:T(1024)} %convert_element_type.284) | copy-start | bytes 9220
  197.3 33.7 %copy-start.46 = (f32[768]{0:T(1024)S(1)}, f32[768]{0:T(1024)}, u32[]{:S(2)}) copy-start(f32[768]{0:T(1024)} %convert_element_type.288) | copy-start | bytes 9220
  230.9 5.4 copy-start.61
  231.0 5.3 copy-start.2
  231.0 5.3 copy-start.27
  259.0 11.3 %copy-start.35 = (f32[1024]{0:T(1024)S(1)}, f32[1024]{0:T(1024)}, u32[]{:S(2)}) copy-start(f32[1024]{0:T(1024)} %copy-done.34) | copy-start | bytes 12292
  271.2 3.2 copy-start.17
  276.8 2.7 copy-start.23
  279.4 192.9 %reduce-scatter.5.cloned.1.call-start = ((), (), s32[]{:S(2)}) async-start(), calls=%async_computation.4 | async-start | bytes 4423680 | tf_op jit(solution)/shard_map/reduce_scatter | solution.py:101
  279.5 5.6 copy-start.26
  279.5 5.7 copy-start.50
  285.2 117.9 %copy-start.37 = (f32[1024]{0:T(1024)S(1)}, f32[1024]{0:T(1024)}, u32[]{:S(2)}) copy-start(f32[1024]{0:T(1024)} %copy-done.36) | copy-start | bytes 12292
  285.2 117.9 %copy-start.39 = (f32[1024]{0:T(1024)S(1)}, f32[1024]{0:T(1024)}, u32[]{:S(2)}) copy-start(f32[1024]{0:T(1024)} %copy-done.38) | copy-start | bytes 12292
  403.0 6.3 copy-start.6
  409.4 3.2 copy-start.13
  423.6 91.5 %reduce-scatter.11.cloned.1.call-start = ((), (), s32[]{:S(2)}) async-start(), calls=%async_computation.7 | async-start | bytes 5898240 | tf_op jit(solution)/shard_map/reduce_scatter | solution.py:110
  439.6 126.0 %reduce-scatter.9.cloned.1.call-start = ((), (), s32[]{:S(2)}) async-start(), calls=%async_computation.6 | async-start | bytes 5898240 | tf_op jit(solution)/shard_map/reduce_scatter | solution.py:107
  472.2 97.1 %copy-start.60 = (bf16[192]{0:T(256)(128)(2,1)S(1)}, bf16[192]{0:T(256)(128)(2,1)}, u32[]{:S(2)}) copy-start(bf16[192]{0:T(256)(128)(2,1)} %param.32) | copy-start | bytes 1156
  472.2 238.5 %all-reduce.21.cloned.1.call-start = ((), (), s32[]{:S(2)}) async-start(), calls=%async_computation.12 | async-start | bytes 7077888 | tf_op jit(solution)/shard_map/psum | solution.py:140
  569.5 4.0 copy-start.44
  569.5 4.0 copy-start.45
  710.7 3.1 copy-start.18
  710.7 4.7 copy-start.20
  713.8 2.9 copy-start.21
  (9 other events, 14.3 us)
Sparse Core Ops, SparseCore 0:
  9.7 20.3 all-gather.11
  31.6 30.7 all-gather.9
  64.0 37.4 all-gather.15
  102.9 37.4 all-gather.13
  279.5 26.1 reduce-scatter.6
  423.7 40.8 reduce-scatter.4
  467.2 47.8 reduce-scatter.10
  517.7 47.8 reduce-scatter.8
  569.6 141.0 all-reduce.20
where the time goes:
time: 731 us; the launch traced here: 725 us
  matrix products  286 us (39%)
  waiting for transfers between devices  195 us (27%)
  local copies, waits for them, and re-layouts  119 us (16%)
  blocking collectives  52.9 us (7%)
  other arithmetic  51.9 us (7%)
  between operations  18.4 us (3%)
    psum x1, waiting for transfers between devices, reduce_grads(): lax.psum(blocks[0].astype(jnp.bfloat16), 'dp').astype(jnp.float32)  81.4 us
    reduce_scatter x1, waiting for transfers between devices, reduce_grads(): lax.psum_scatter(grads[2].astype(jnp.bfloat16), ('mx', 'my'), scatter_dim...  50.6 us
    dot_general x4, matrix products, project_forward(): jnp.einsum('tid,ijdn->tjn', operand.reshape(rows_here, grid_rows, row_siz...  45.6 us
    dot_general x4, matrix products, project_back(): jnp.einsum('tjn,ijdn->tid', grad_rows.reshape(rows_here, grid_cols, col_s...  42.9 us
    reduce_scatter x1, waiting for transfers between devices, reduce_grads(): lax.psum_scatter(grads[3].astype(jnp.bfloat16), ('mx', 'my'), scatter_dim...  42.8 us
    dot_general x12, matrix products, attend_back(): jnp.einsum('sij,sid->sjd', scores.astype(jnp.bfloat16), numer_grad, prefe...  33.9 us
    reshape x6, local copies, waits for them, and re-layouts, fetch_weights(): piece.reshape(grid_rows, grid_cols, piece.shape[1], piece.shape[2])  32.3 us
    dot_general x12, matrix products, attend_back(): jnp.einsum('sij,sjd->sid', score_grad, k_part, preferred_element_type=jnp...  31.1 us
  transfers between devices with their start and end apart: 9, of which 4 were waited for; matrix products, arithmetic and copies ran while one was open for 48% of the time, Pallas kernels for 0%

commit v1 on v0

--- a/solution.py
+++ b/solution.py
@@ -6,6 +6,12 @@
 
 HD = 64
 norm_eps = 1e-05
+
+
+def gather_and_add(x, axis):
+    blocks = lax.all_gather(x, axis, axis=0, tiled=False)
+    total = blocks.sum(axis=0)
+    return total
 
 
 def layer_norm(resid, gain, shift):
@@ -137,7 +143,7 @@
     )
     blocks = tuple((piece[0] for piece in summed[:4])) + tuple(summed[4:])
     return (
-        lax.psum(blocks[0].astype(jnp.bfloat16), "dp").astype(jnp.float32),
+        gather_and_add(blocks[0].astype(jnp.bfloat16), "dp").astype(jnp.float32),
         lax.psum(blocks[1].astype(jnp.bfloat16), "dp").astype(jnp.float32),
         lax.psum(blocks[2].astype(jnp.bfloat16), "dp").astype(jnp.float32),
         lax.psum(blocks[3].astype(jnp.bfloat16), "dp").astype(jnp.float32),

time: 731 us -> 768 us (1.051)
  waiting for transfers between devices: 195 us -> 226 us
    all_gather x0 -> x1, waiting for transfers between devices: none -> 104 us  [gather_and_add(): blocks = lax.all_gather(x, axis, axis=0, tiled=False)]
    reduce_scatter x1, waiting for transfers between devices: 50.6 us -> 0.02 us  [reduce_grads(): lax.psum_scatter(grads[2].astype(jnp.bfloat16), ('mx', 'my'), scatter_dim...]
    reduce_scatter x1, waiting for transfers between devices: 42.8 us -> 0.02 us  [reduce_grads(): lax.psum_scatter(grads[3].astype(jnp.bfloat16), ('mx', 'my'), scatter_dim...]
    reduce_scatter x1, waiting for transfers between devices: 0.02 us -> 40.2 us  [reduce_grads(): lax.psum_scatter(grads[0].astype(jnp.bfloat16), ('mx', 'my'), scatter_dim...]
    psum x1, waiting for transfers between devices: 81.4 us -> 58.1 us  [reduce_grads(): lax.psum(blocks[1].astype(jnp.bfloat16), 'dp').astype(jnp.float32)]
    unnamed x160 -> x154, local copies, waits for them, and re-layouts: 31.1 us -> 29.4 us
  transfers between devices with their start and end apart: 9 -> 10, of which waited for: 4 -> 4; matrix products, arithmetic and copies ran while one was open for 48% -> 47% of each run, Pallas kernels for 0% -> 0%
where the time goes in v1:
time: 768 us; the launch traced here: 761 us
  matrix products  287 us (37%)
  waiting for transfers between devices  226 us (29%)
  local copies, waits for them, and re-layouts  118 us (15%)
  other arithmetic  58.3 us (8%)
  blocking collectives  52.6 us (7%)
  between operations  18.5 us (2%)
    all_gather x1, waiting for transfers between devices, gather_and_add(): blocks = lax.all_gather(x, axis, axis=0, tiled=False)  104 us
    psum x1, waiting for transfers between devices, reduce_grads(): lax.psum(blocks[1].astype(jnp.bfloat16), 'dp').astype(jnp.float32)  58.1 us
    dot_general x4, matrix products, project_forward(): jnp.einsum('tid,ijdn->tjn', operand.reshape(rows_here, grid_rows, row_siz...  45.5 us
    dot_general x4, matrix products, project_back(): jnp.einsum('tjn,ijdn->tid', grad_rows.reshape(rows_here, grid_cols, col_s...  43 us
    reduce_scatter x1, waiting for transfers between devices, reduce_grads(): lax.psum_scatter(grads[0].astype(jnp.bfloat16), ('mx', 'my'), scatter_dim...  40.2 us
    dot_general x12, matrix products, attend_back(): jnp.einsum('sij,sid->sjd', scores.astype(jnp.bfloat16), numer_grad, prefe...  34 us
    reshape x6, local copies, waits for them, and re-layouts, fetch_weights(): piece.reshape(grid_rows, grid_cols, piece.shape[1], piece.shape[2])  32.3 us
    dot_general x12, matrix products, attend_back(): jnp.einsum('sij,sjd->sid', score_grad, k_part, preferred_element_type=jnp...  31.1 us
  transfers between devices with their start and end apart: 10, of which 4 were waited for; matrix products, arithmetic and copies ran while one was open for 47% of the time, Pallas kernels for 0%

profile of v1, /device:TPU:0, one launch (start us, length us, event | category | flops | bytes accessed | tf_op | source)
XLA Modules:
  0.0 761.2 jit_solution(16829244715967930198)
XLA Ops:
  13.5 13.2 %all-reduce.18 = (bf16[2304]{0:T(1024)(128)(2,1)S(1)}, bf16[768]{0:T(1024)(128)(2,1)S(1)}, bf16[768]{0:T(1024)(128)(2,1)S(1)}, bf16[768]{0:T(1024)(128)(2,1)S(1)...) all-reduce(bf16[2304]{0:T(1024)(128)(2,1)S(1)} %dynamic-update-slic, ...), channel_id=1, replica_groups=mesh['dp'=8,'mx'=2,'my'=2] {'mx','my'}, use_global_device_ids=true, to_apply=%add | all-reduce | flops 6144 | bytes 24576
  30.9 5.2 all-gather.4
  42.3 20.1 %all-gather.13.cloned.1.call-done = bf16[1536,1152]{1,0:T(8,128)(2,1)} async-done(((bf16[384,1152]{1,0:T(8,128)(2,1)}), bf16[1536,1152]{1,0:T(8,128)(2,1)}) %all-gather.13.cloned.1.call-update) | async-done | bytes 3538960 | tf_op jit(solution)/shard_map/all_gather | solution.py:81
  62.4 4.5 copy.202
  66.9 5.3 bitcast_add_fusion.1
  72.2 3.3 slice_maximum_fusion
  81.6 3.5 copy.204
  85.2 4.7 fusion.106
  90.3 2.8 copy.208
  95.6 2.8 copy.207
  100.1 2.8 copy.209
  102.9 53.0 %while.30 = (s32[]{:T(128)}, f32[12,1,1024,64]{2,3,1,0:T(8,128)}, f32[12,1,1024]{2,1,0:T(1,128)S(1)}, bf16[12,1,1024,128]{3,2,1,0:T(8,128)(2,1)}, bf16[12,1,1024...) while((s32[]{:T(128)}, f32[12,1,1024,64]{2,3,1,0:T(8,128)}, ...), condition=%wide.region_3.4_spmd.clone.clone, body=%wide.region_1.3_spmd.clone.sunk.clone | while | flops 415236096 | bytes 9476177 | solution.py:236
  162.3 7.3 copy.215
  169.5 4.9 copy.219
  174.5 6.6 copy.213
  181.1 4.9 copy.221
  186.1 33.6 %multiply_convert_fusion = (bf16[1024,3072]{1,0:T(8,128)(2,1)S(1)}, f32[1024,3072]{1,0:T(8,128)}, f32[1024,3072,1]{1,0,2:T(8,128)}) fusion(f32[3072]{0:T(1024)S(1)} %bitcast.426, bf16[1024,2,384]{0,2,1:T(8,128)(2,1)S(1)} %bitcast.411, bf16[3072,384,2]{1,0,2:T(8,128)(2,1)S(1)} %bitcast.399), kind=kOutput, calls=%fused_computation.69 | convolution fusion | flops 5039456256 | bytes 37761024 | tf_op jit(solution)/shard_map/tid,ijdn->tjn/dot_general | solution.py:44
  219.8 5.3 fusion.127
  228.1 2.9 fusion.120
  231.0 16.8 %fusion.128 = (bf16[3072]{0:T(1024)(128)(2,1)S(1)}, bf16[1024,3072]{1,0:T(8,128)(2,1)}) fusion(f32[1024,3072]{1,0:T(8,128)} %get-tuple-element.375, bf16[1024,2,384]{0,2,1:T(8,128)(2,1)} %bitcast.415, bf16[3072,2,384]{2,0,1:T(8,128)(2,1)} %bitcast.395, f32[3072]{0:T(1024)S(1)} %bitcast.427, f32[1024,3072,1]{1,0,2:T(8,128)} %get-tuple-element.400), kind=kOutput, calls=%fused_computation.190 | convolution fusion | flops 4882166784 | bytes 37767168 | tf_op jit(solution)/shard_map/tjn,ijdn->tid/dot_general | solution.py:56
  247.8 11.2 %multiply_reduce_fusion = (bf16[768]{0:T(1024)(128)(2,1)S(1)}, f32[1024]{0:T(1024)S(1)}, bf16[768]{0:T(1024)(128)(2,1)S(1)}, f32[1024,768]{0,1:T(8,128)S(1)}) fusion(f32[1024,768]{0,1:T(8,128)S(1)} %copy-done.1, f32[1024]{0:T(1024)S(1)} %copy-done.30, f32[1024]{0:T(1024)S(1)} %copy-done.26, f32[768]{0:T(1024)S(1)} %copy-done.28, ...), kind=kOutput, calls=%fused_computation.135 | convolution fusion | flops 4845204480 | bytes 22057984 | tf_op jit(solution)/shard_map/tjn,ijdn->tid/dot_general | solution.py:56
  265.5 2.6 copy.239
  268.2 9.1 %convert_bitcast_fusion = bf16[2,2,1536,384]{2,3,0,1:T(8,128)(2,1)} fusion(bf16[1024,2,384,1]{0,2,3,1:T(8,128)(2,1)} %bitcast.416, bf16[128,2,8,1536]{3,2,1,0:T(8,128)(2,1)} %bitcast.430), kind=kOutput, calls=%fused_computation.99 | convolution fusion | flops 4834197504 | bytes 12582912 | tf_op jit(solution)/shard_map/tid,tjn->ijdn/dot_general | solution.py:68
  277.3 6.7 copy.244
  287.8 4.8 slice_compare_fusion.1
  292.7 2.7 copy.217
  295.4 2.7 copy.231
  298.1 15.1 %reshape.596 = bf16[1024,2,1536]{2,1,0:T(2,128)(2,1)} reshape(bf16[1024,3072]{1,0:T(8,128)(2,1)} %get-tuple-element.405) | data formatting | bytes 12582912 | tf_op jit(solution)/shard_map/reshape | solution.py:58
  313.3 10.6 %convert_bitcast_fusion.1 = bf16[2,2,384,1536]{2,3,0,1:T(8,128)(2,1)} fusion(bf16[1024,2,384,1]{0,2,1,3:T(8,128)(2,1)} %bitcast.412, bf16[1024,2,1536,1]{2,1,0,3:T(2,128)(2,1)} %bitcast.385), kind=kOutput, calls=%fused_computation.100 | convolution fusion | flops 4834197504 | bytes 12582912 | tf_op jit(solution)/shard_map/tid,tjn->ijdn/dot_general | solution.py:68
  323.9 6.7 copy.242
  330.6 5.7 fusion.97
  336.9 118.5 %while.31 = (s32[]{:T(128)}, f32[12,1,1024,128]{2,3,0,1:T(8,128)}, f32[12,1,1024,128]{2,3,0,1:T(8,128)}, bf16[12,1,1024,64]{2,3,1,0:T(8,128)(2,1)}, bf16[12,1,10...) while((s32[]{:T(128)}, f32[12,1,1024,128]{2,3,0,1:T(8,128)}, ...), condition=%wide.region_14.15_spmd.clone.clone, body=%wide.region_13.14_spmd.clone.sunk.clone | while | flops 1088421888 | bytes 9208937 | solution.py:289
  344.3 2.9 fusion.196
  349.3 2.6 fusion.194
  354.2 2.9 fusion.196
  364.1 2.8 fusion.196
  374.0 2.8 fusion.196
  379.0 2.6 fusion.194
  383.9 2.8 fusion.196
  393.7 2.8 fusion.196
  403.4 2.8 fusion.196
  408.4 2.6 fusion.194
  413.3 2.8 fusion.196
  418.3 2.6 fusion.194
  423.1 2.8 fusion.196
  428.1 2.6 fusion.194
  432.9 2.8 fusion.196
  437.9 2.6 fusion.194
  442.7 2.8 fusion.196
  447.7 2.6 fusion.194
  452.6 2.8 fusion.196
  455.4 6.3 fusion.95
  464.8 5.3 fusion.84
  470.0 5.8 copy.237
  476.6 40.2 %reduce-scatter.5.cloned.1.call-done = bf16[1,384,1152]{2,1,0:T(8,128)(2,1)} async-done(((bf16[4,384,1152]{2,1,0:T(8,128)(2,1)}), bf16[1,384,1152]{2,1,0:T(8,128)(2,1)}) %reduce-scatter.5.cloned.1.call-update) | async-done | bytes 884752 | tf_op jit(solution)/shard_map/reduce_scatter | solution.py:107
  520.8 4.1 copy.233
  524.9 10.7 %all-reduce.17 = (bf16[768]{0:T(1024)(128)(2,1)S(1)}, bf16[2304]{0:T(1024)(128)(2,1)S(1)}, bf16[768]{0:T(1024)(128)(2,1)S(1)}, bf16[768]{0:T(1024)(128)(2,1)S(1)...) all-reduce(bf16[768]{0:T(1024)(128)(2,1)S(1)} %dynamic-update-slice, ...), channel_id=1, replica_groups=mesh['dp'=8,'mx'=2,'my'=2] {'mx','my'}, use_global_device_ids=true, to_apply=%add.6 | all-reduce | flops 10752 | bytes 43008
  536.2 23.6 %all-reduce.15 = (bf16[576]{0:T(1024)(128)(2,1)S(1)}, bf16[192]{0:T(256)(128)(2,1)S(1)}, bf16[192]{0:T(256)(128)(2,1)S(1)}, bf16[192]{0:T(256)(128)(2,1)S(1)}, b...) all-reduce(bf16[576]{0:T(1024)(128)(2,1)S(1)} %dynamic-slice.8, ...), channel_id=1, replica_groups=mesh['dp'=8,'mx'=2,'my'=2] {'dp'}, use_global_device_ids=true, to_apply=%region_19.20 | all-reduce | flops 2496 | bytes 9984 | tf_op jit(solution)/shard_map/psum | solution.py:150
  564.3 9.3 %fusion.98 = bf16[1024,768]{0,1:T(8,128)(2,1)} fusion(f32[1024,768]{0,1:T(8,128)} %copy-done.4, bf16[768,2,1152]{2,0,1:T(8,128)(2,1)} %bitcast.403, bf16[1024,2,1152]{0,2,1:T(8,128)(2,1)} %bitcast.393, f32[1024]{0:T(1024)S(1)} %negate_multiply_fusion.1), kind=kOutput, calls=%fused_computation.128 | convolution fusion | flops 3626237952 | bytes 12980224 | tf_op jit(solution)/shard_map/tjn,ijdn->tid/dot_general | solution.py:56
  573.6 2.6 copy.246
  580.4 58.1 %all-reduce.21.cloned.1.call-done = (bf16[384,384]{1,0:T(8,128)(2,1)}, bf16[384,1536]{1,0:T(8,128)(2,1)}, bf16[1536,384]{1,0:T(8,128)(2,1)}) async-done(((bf16[384,384]{1,0:T(8,128)(2,1)}, bf16[384,1536]{1,0:T(8,128)(2,1)}, bf16[1536,384]{1,0:T(8,128)(2,1)}), (bf16[384,384]{1,0:T(8,128)(2,1)}, bf16[384,1536]{1,0:T(8,128)(2,1)}, bf16[1536,384]{1,0:T(8,128)(2,1)})) %all-reduce.21.cloned.1.call-update) | async-done | bytes 2654224 | tf_op jit(solution)/shard_map/psum | solution.py:147
  638.5 3.1 convert_element_type.318
  644.0 104.4 %all-gather.11.cloned.1.call-done = bf16[8,384,1152]{2,1,0:T(8,128)(2,1)} async-done(((bf16[1,384,1152]{2,1,0:T(8,128)(2,1)}), bf16[8,384,1152]{2,1,0:T(8,128)(2,1)}) %all-gather.11.cloned.1.call-update) | async-done | bytes 7077904 | tf_op jit(solution)/shard_map/all_gather | solution.py:12
  748.4 4.5 reduce_sum.240
  (320 shorter events, 183.6 us)
Async XLA Ops:
  7.2 3.0 copy-start.48
  7.2 4.9 copy-start.52
  7.2 5.2 copy-start.53
  7.2 5.4 copy-start.54
  7.2 5.6 copy-start.55
  7.2 5.8 copy-start.56
  7.2 6.1 copy-start.49
  7.3 20.1 %copy-start.51 = (s32[1,8]{1,0:T(1,128)S(1)}, s32[1,8]{1,0:T(1,128)}, u32[]{:S(2)}) copy-start(s32[1,8]{1,0:T(1,128)} %param.34) | copy-start | bytes 100
  7.3 20.1 %copy-start.45 = (s32[1024]{0:T(1024)S(1)}, s32[1024]{0:T(1024)}, u32[]{:S(2)}) copy-start(s32[1024]{0:T(1024)} %param.33) | copy-start | bytes 12292
  7.3 21.4 %copy-start.10 = (bf16[1024,768]{1,0:T(8,128)(2,1)S(1)}, bf16[1024,768]{1,0:T(8,128)(2,1)}, u32[]{:S(2)}) copy-start(bf16[1024,768]{1,0:T(8,128)(2,1)} %param.20) | copy-start | bytes 4718596
  7.3 32.5 %all-gather.15.cloned.1.call-start = ((), (), s32[]{:S(2)}) async-start(), calls=%async_computation.10 | async-start | bytes 1474560 | tf_op jit(solution)/shard_map/all_gather | solution.py:82
  8.0 22.9 %copy-start.50 = (bf16[768]{0:T(1024)(128)(2,1)S(1)}, bf16[768]{0:T(1024)(128)(2,1)}, u32[]{:S(2)}) copy-start(bf16[768]{0:T(1024)(128)(2,1)} %param.28) | copy-start | bytes 4612
  8.0 29.8 %copy-start.5 = (bf16[1024,768]{1,0:T(8,128)(2,1)S(1)}, bf16[1024,768]{1,0:T(8,128)(2,1)}, u32[]{:S(2)}) copy-start(bf16[1024,768]{1,0:T(8,128)(2,1)} %param.35) | copy-start | bytes 4718596
  8.0 54.4 %all-gather.13.cloned.1.call-start = ((), (), s32[]{:S(2)}) async-start(), calls=%async_computation.9 | async-start | bytes 4423680 | tf_op jit(solution)/shard_map/all_gather | solution.py:81
  8.8 153.5 %all-gather.19.cloned.1.call-start = ((), (), s32[]{:S(2)}) async-start(), calls=%async_computation.12 | async-start | bytes 5898240 | tf_op jit(solution)/shard_map/all_gather | solution.py:84
  9.5 164.9 %all-gather.17.cloned.1.call-start = ((), (), s32[]{:S(2)}) async-start(), calls=%async_computation.11 | async-start | bytes 5898240 | tf_op jit(solution)/shard_map/all_gather | solution.py:83
  10.1 465.8 %reduce-scatter.7.cloned.1.call-start = ((), (), s32[]{:S(2)}) async-start(), calls=%async_computation.6 | async-start | bytes 1474560 | tf_op jit(solution)/shard_map/reduce_scatter | solution.py:110
  28.1 57.1 %copy-start.33 = (f32[1024]{0:T(1024)}, f32[1024]{0:T(1024)S(1)}, u32[]{:S(2)}) copy-start(f32[1024]{0:T(1024)S(1)} %get-tuple-element.392) | copy-start | bytes 12292
  28.1 57.1 %copy-start.35 = (f32[1024]{0:T(1024)}, f32[1024]{0:T(1024)S(1)}, u32[]{:S(2)}) copy-start(f32[1024]{0:T(1024)S(1)} %get-tuple-element.395) | copy-start | bytes 12292
  30.3 130.2 %copy-start.27 = (f32[768]{0:T(1024)}, f32[768]{0:T(1024)S(1)}, u32[]{:S(2)}) copy-start(f32[768]{0:T(1024)S(1)} %convert_element_type.283) | copy-start | bytes 9220
  72.2 5.7 copy-start.3
  81.6 3.6 copy-start.37
  100.1 2.8 copy-start.21
  100.1 2.8 copy-start.46
  155.8 4.2 copy-start.22
  155.8 2.6 copy-start.12
  155.9 2.7 copy-start.17
  155.9 2.7 copy-start.44
  155.9 2.5 copy-start.19
  160.5 9.1 %copy-start.31 = (f32[1024]{0:T(1024)}, f32[1024]{0:T(1024)S(1)}, u32[]{:S(2)}) copy-start(f32[1024]{0:T(1024)S(1)} %multiply_reduce_fusion.3) | copy-start | bytes 12292
  161.7 7.8 %copy-start.29 = (f32[1024]{0:T(1024)}, f32[1024]{0:T(1024)S(1)}, u32[]{:S(2)}) copy-start(f32[1024]{0:T(1024)S(1)} %fusion.115) | copy-start | bytes 12292
  162.2 23.8 %copy-start.13 = (bf16[1024,768]{0,1:T(8,128)(2,1)}, bf16[1024,768]{0,1:T(8,128)(2,1)S(1)}, u32[]{:S(2)}) copy-start(bf16[1024,768]{0,1:T(8,128)(2,1)S(1)} %fusion.101) | copy-start | bytes 4718596
  181.1 4.9 copy-start.8
  181.1 4.9 copy-start.40
  181.1 38.6 %slice-start = ((s8[4718592]{0:T(1024)(128)(4,1)}), s8[524288]{0:T(1024)(128)(4,1)S(1)}, s32[]{:S(2)}) async-start(s8[4718592]{0:T(1024)(128)(4,1)} %bitcast.396), calls=%async_computation.14 | async-start | bytes 1048576
  186.0 33.7 %copy-start.1 = (f32[1024,768]{0,1:T(8,128)S(1)}, f32[1024,768]{0,1:T(8,128)}, u32[]{:S(2)}) copy-start(f32[1024,768]{0,1:T(8,128)} %copy-done) | copy-start | bytes 9437188
  186.0 33.7 %slice-start.1 = ((s8[4718592]{0:T(1024)(128)(4,1)}), s8[4194304]{0:T(1024)(128)(4,1)S(1)}, s32[]{:S(2)}) async-start(s8[4718592]{0:T(1024)(128)(4,1)} %bitcast.396), calls=%async_computation.15 | async-start | bytes 8388608
  186.0 33.7 %copy-start.26 = (f32[1024]{0:T(1024)S(1)}, f32[1024]{0:T(1024)}, u32[]{:S(2)}) copy-start(f32[1024]{0:T(1024)} %copy-done.25) | copy-start | bytes 12292
  186.1 33.7 %copy-start.28 = (f32[768]{0:T(1024)S(1)}, f32[768]{0:T(1024)}, u32[]{:S(2)}) copy-start(f32[768]{0:T(1024)} %copy-done.27) | copy-start | bytes 9220
  186.1 33.7 %copy-start.30 = (f32[1024]{0:T(1024)S(1)}, f32[1024]{0:T(1024)}, u32[]{:S(2)}) copy-start(f32[1024]{0:T(1024)} %copy-done.29) | copy-start | bytes 12292
  186.1 33.7 %copy-start.39 = (f32[768]{0:T(1024)S(1)}, f32[768]{0:T(1024)}, u32[]{:S(2)}) copy-start(f32[768]{0:T(1024)} %convert_element_type.284) | copy-start | bytes 9220
  186.1 33.7 %copy-start.43 = (f32[768]{0:T(1024)S(1)}, f32[768]{0:T(1024)}, u32[]{:S(2)}) copy-start(f32[768]{0:T(1024)} %convert_element_type.288) | copy-start | bytes 9220
  219.7 5.4 copy-start.58
  219.8 5.3 copy-start.2
  219.8 5.3 copy-start.24
  247.8 11.2 %copy-start.32 = (f32[1024]{0:T(1024)S(1)}, f32[1024]{0:T(1024)}, u32[]{:S(2)}) copy-start(f32[1024]{0:T(1024)} %copy-done.31) | copy-start | bytes 12292
  259.9 3.2 copy-start.15
  268.2 207.8 %reduce-scatter.11.cloned.1.call-start = ((), (), s32[]{:S(2)}) async-start(), calls=%async_computation.8 | async-start | bytes 5898240 | tf_op jit(solution)/shard_map/reduce_scatter | solution.py:116
  284.0 191.9 %reduce-scatter.9.cloned.1.call-start = ((), (), s32[]{:S(2)}) async-start(), calls=%async_computation.7 | async-start | bytes 5898240 | tf_op jit(solution)/shard_map/reduce_scatter | solution.py:113
  323.9 6.7 copy-start.20
  330.6 5.7 copy-start.23
  336.4 180.5 %reduce-scatter.5.cloned.1.call-start = ((), (), s32[]{:S(2)}) async-start(), calls=%async_computation.4 | async-start | bytes 4423680 | tf_op jit(solution)/shard_map/reduce_scatter | solution.py:107
  336.9 118.5 %copy-start.34 = (f32[1024]{0:T(1024)S(1)}, f32[1024]{0:T(1024)}, u32[]{:S(2)}) copy-start(f32[1024]{0:T(1024)} %copy-done.33) | copy-start | bytes 12292
  336.9 118.5 %copy-start.36 = (f32[1024]{0:T(1024)S(1)}, f32[1024]{0:T(1024)}, u32[]{:S(2)}) copy-start(f32[1024]{0:T(1024)} %copy-done.35) | copy-start | bytes 12292
  455.4 6.3 copy-start.6
  461.7 3.1 copy-start.11
  462.6 2.1 copy-start.7
  475.8 44.7 %copy-start.57 = (bf16[192]{0:T(256)(128)(2,1)S(1)}, bf16[192]{0:T(256)(128)(2,1)}, u32[]{:S(2)}) copy-start(bf16[192]{0:T(256)(128)(2,1)} %param.32) | copy-start | bytes 1156
  475.9 162.6 %all-reduce.21.cloned.1.call-start = ((), (), s32[]{:S(2)}) async-start(), calls=%async_computation.13 | async-start | bytes 5308416 | tf_op jit(solution)/shard_map/psum | solution.py:147
  476.6 271.8 %all-gather.11.cloned.1.call-start = ((), (), s32[]{:S(2)}) async-start(), calls=%async_computation.5 | async-start | bytes 7962624 | tf_op jit(solution)/shard_map/all_gather | solution.py:12
  520.8 4.1 copy-start.41
  520.8 4.1 copy-start.42
  638.5 3.1 copy-start.16
  638.5 4.6 copy-start.18
  (7 other events, 10.2 us)
Sparse Core Ops, SparseCore 0:
  9.7 20.2 all-gather.14
  31.6 30.7 all-gather.12
  64.0 37.4 all-gather.18
  102.9 37.4 all-gather.16
  268.3 26.0 reduce-scatter.6
  297.0 47.7 reduce-scatter.10
  347.3 47.8 reduce-scatter.8
  476.0 40.8 reduce-scatter.4
  520.9 117.5 all-reduce.20
  640.5 107.7 all-gather.10
